TPU v7x, 32 devices: a whole 2x2x4 slice. The times are simulated.
32 devices in a mesh: slab: 8 (over z, y), patch: 4 (over x, core).
Axes of the slice: x: 2, y: 2, z: 4, core: 2. Of those that a mesh axis runs over, the one named last changes fastest.
Arguments:
- fluid_state: float32 [16, 256, 256], P('slab', 'patch'), may hold values from -6 to 6
- fluid_rhs: float32 [16, 256, 256], P('slab', 'patch'), may hold values from -24 to 24
- element_scale: float32 [16, 256], P('slab', 'patch'), may hold values from 1 to 4
- element_matrix: bfloat16 [256, 256], replicated
- couple_x: bfloat16 [256, 256], replicated, may hold values from -0.09375 to 0.09375
- couple_y: bfloat16 [256, 256], replicated, may hold values from -0.09375 to 0.09375
- block_inverse: bfloat16 [256, 256], replicated
- traction_map: bfloat16 [3, 256], replicated, may hold values from -0.375 to 0.375
- slot_elem: int32 [8, 4, 1024], P('slab', 'patch'), may hold values from 0 to 127
- slot_point: int32 [8, 4, 1024], P('slab', 'patch'), may hold values from 0 to 8191
- slot_count: int32 [8, 4, 4], P('slab', 'patch'), may hold values from 0 to 256, as said below
- displacement: float32 [3, 256, 128], P(None, 'patch'), may hold values from -6 to 6
- stiffness: float32 [256, 128], P('patch'), may hold values from 0.03 to 0.3
Outputs:
- fluid_out: float32 [16, 256, 256], P('slab', 'patch')
- displacement_new: float32 [3, 256, 128], P(None, 'patch')
- wall_motion: float32 [3, 8, 4, 1024], P(None, 'slab', 'patch')
Inputs may be any that keep to these rules, and one draw needn't show every extreme that they name: For every block and owner only the first slot_count slots of that owner's 256 slots are live; the count 256 is reached for some block and owner in every draw.
All inputs are finite; a program needn't handle non-finite values.
Results may differ from a plain program's by a relative error of at most 0.0049.
Values may be sent and summed in bfloat16 or wider, within the bound.
A program may use at most 128 MiB of HBM per device.

v0:
```python
import jax
import jax.numpy as jnp
from jax import lax
from jax.sharding import PartitionSpec as P

SWEEPS = 3


def with_halo(cells, sides, width):
    for axis, dim in sides:
        count = lax.axis_size(axis)
        ends = count - 1
        head = lax.slice_in_dim(cells, 0, width, axis=dim)
        tail = lax.slice_in_dim(cells, cells.shape[dim] - width, cells.shape[dim], axis=dim)
        cells = jnp.concatenate(
            [
                lax.ppermute(tail, axis, [(i, (i + 1) % count) for i in range(ends)]),
                cells,
                lax.ppermute(head, axis, [((i + 1) % count, i) for i in range(ends)]),
            ],
            axis=dim,
        )
    return cells


def element_apply(rounded, scale, element_matrix, couple_x, couple_y):
    padded = with_halo(rounded, (("slab", 0), ("patch", 1)), 1)
    along_x = (padded[:-2, 1:-1].astype(jnp.float32) + padded[2:, 1:-1].astype(jnp.float32)).astype(
        jnp.bfloat16
    )
    along_y = (padded[1:-1, :-2].astype(jnp.float32) + padded[1:-1, 2:].astype(jnp.float32)).astype(
        jnp.bfloat16
    )
    width = rounded.shape[2]
    own = jnp.dot(rounded.reshape(-1, width), element_matrix, preferred_element_type=jnp.float32)
    side_x = jnp.dot(along_x.reshape(-1, width), couple_x, preferred_element_type=jnp.float32)
    side_y = jnp.dot(along_y.reshape(-1, width), couple_y, preferred_element_type=jnp.float32)
    return (
        scale[:, :, None] * own.reshape(rounded.shape)
        - side_x.reshape(rounded.shape)
        - side_y.reshape(rounded.shape)
    )


def laplace_net(field):
    edged = with_halo(field.astype(jnp.bfloat16), (("patch", 1),), 1).astype(field.dtype)
    edged = jnp.pad(edged, ((0, 0), (0, 0), (1, 1)))
    return 4.0 * field - (
        edged[:, 2:, 1:-1] + edged[:, :-2, 1:-1] + edged[:, 1:-1, 2:] + edged[:, 1:-1, :-2]
    )


def shards(
    fluid_state,
    fluid_rhs,
    element_scale,
    element_matrix,
    couple_x,
    couple_y,
    block_inverse,
    traction_map,
    slot_elem,
    slot_point,
    slot_count,
    displacement,
    stiffness,
):
    width = fluid_state.shape[2]
    state = fluid_state
    for sweep in range(SWEEPS):
        rounded = state.astype(jnp.bfloat16)
        applied = element_apply(rounded, element_scale, element_matrix, couple_x, couple_y)
        residue = (fluid_rhs - applied).astype(jnp.bfloat16)
        update = jnp.dot(
            residue.reshape(-1, width), block_inverse, preferred_element_type=jnp.float32
        ).reshape(state.shape)
        state = state + update / element_scale[:, :, None]
    final = state.astype(jnp.bfloat16)
    owners = lax.axis_size("patch")
    capacity = slot_elem.shape[2] // owners
    net_rows = displacement.shape[1]
    net_cols = displacement.shape[2]
    cells = net_rows * net_cols
    rows = jnp.take(final.reshape(-1, width), slot_elem.reshape(-1), axis=0).reshape(
        owners, capacity, width
    )
    pull = jnp.einsum("cd,kqd->kcq", traction_map, rows, preferred_element_type=jnp.float32)
    limits = slot_count.reshape(owners)
    live = (lax.broadcasted_iota(jnp.int32, (owners, capacity), 1) < limits[:, None]).astype(
        jnp.float32
    )
    pull = pull * live[:, None, :]
    points = slot_point.reshape(owners, capacity)
    owner_ids = lax.broadcasted_iota(jnp.int32, (owners, capacity), 0)
    got_pull, got_points = (
        lax.all_to_all(pull, "patch", split_axis=0, concat_axis=0, tiled=True),
        lax.all_to_all(points, "patch", split_axis=0, concat_axis=0, tiled=True),
    )
    local = jnp.zeros((3, cells), jnp.float32)
    local = local.at[:, got_points.reshape(-1)].add(got_pull.transpose(1, 0, 2).reshape(3, -1))
    loads = lax.psum(local, "slab")
    loads = loads.reshape(3, net_rows, net_cols)
    bend = laplace_net(displacement)
    stiff_term = stiffness[None] * (laplace_net(bend) + 4.0 * bend)
    displacement_new = displacement + (loads - stiff_term) / (36.0 * stiffness[None])
    flat_net = displacement_new.reshape(3, -1)
    whole = lax.all_gather(flat_net, "patch", axis=1, tiled=True)
    picked = whole[:, (owner_ids * cells + points).reshape(-1)]
    wall_motion = (picked * live.reshape(1, -1)).reshape(3, 1, 1, owners * capacity)
    return (state, displacement_new, wall_motion)


def solution(mesh):
    return jax.shard_map(
        shards,
        mesh=mesh,
        in_specs=(
            P("slab", "patch", None),
            P("slab", "patch", None),
            P("slab", "patch"),
            P(),
            P(),
            P(),
            P(),
            P(),
            P("slab", "patch", None),
            P("slab", "patch", None),
            P("slab", "patch", None),
            P(None, "patch", None),
            P("patch", None),
        ),
        out_specs=(
            P("slab", "patch", None),
            P(None, "patch", None),
            P(None, "slab", "patch", None),
        ),
        check_vma=False,
    )
```

profile of v0, /device:TPU:0, one launch (start us, length us, event | category | flops | bytes accessed | tf_op | source)
XLA Modules:
  0.0 299.1 jit_solution(18253544204650045127)
XLA Ops:
  8.3 1.3 collective-permute-start.1
  9.6 5.5 %collective-permute-start = (bf16[1,64,256]{2,1,0:T(8,128)(2,1)S(1)}, bf16[1,64,256]{2,1,0:T(8,128)(2,1)S(1)}, u32[]{:S(2)}, u32[]{:S(2)}) collective-permute-start(bf16[1,64,256]{2,1,0:T(8,128)(2,1)S(1)} %get-tuple-element.24), channel_id=1, source_target_pairs={{0,4},{4,8},{8,12},{12,16},{16,20},{20,24},{24,28},{1,5},{5,9},{9,... | collective-permute-start | bytes 98312 | tf_op jit(solution)/shard_map/ppermute | solution.py:17
  15.1 3.3 %all-to-all-start = ((s32[4,1,256]{2,1,0:T(1,128)}), s32[4,1,256]{2,1,0:T(1,128)S(1)}, u32[]{:S(2)}, u32[]{:S(2)}) async-start(s32[4,1,256]{2,1,0:T(1,128)} %bitcast.90), calls=%async_computation | async-start | bytes 8192 | tf_op jit(solution)/shard_map/all_to_all | solution.py:97
  19.3 1.3 collective-permute-start.13
  20.6 3.0 %collective-permute-start.12 = (bf16[3,1,128]{2,1,0:T(2,128)(2,1)S(1)}, bf16[3,1,128]{2,1,0:T(2,128)(2,1)S(1)}, u32[]{:S(2)}, u32[]{:S(2)}) collective-permute-start(bf16[3,1,128]{2,1,0:T(2,128)(2,1)S(1)} %get-tuple-element.28), channel_id=1, source_target_pairs={{0,1},{1,2},{2,3},{4,5},{5,6},{6,7},{8,9},{9,10},{10,11},{12,13},{... | collective-permute-start | bytes 2312 | tf_op jit(solution)/shard_map/ppermute | solution.py:17
  24.9 1.3 reduce.3
  32.0 4.3 %collective-permute-start.14 = (bf16[3,1,128]{2,1,0:T(2,128)(2,1)S(1)}, bf16[3,1,128]{2,1,0:T(2,128)(2,1)S(1)}, u32[]{:S(2)}, u32[]{:S(2)}) collective-permute-start(bf16[3,1,128]{2,1,0:T(2,128)(2,1)S(1)} %get-tuple-element.26), channel_id=1, source_target_pairs={{0,1},{1,2},{2,3},{4,5},{5,6},{6,7},{8,9},{9,10},{10,11},{12,13},{... | collective-permute-start | bytes 2312 | tf_op jit(solution)/shard_map/ppermute | solution.py:17
  36.3 1.3 collective-permute-start.3
  37.6 4.3 %collective-permute-start.2 = (bf16[4,1,256]{2,1,0:T(2,128)(2,1)S(1)}, bf16[4,1,256]{2,1,0:T(2,128)(2,1)S(1)}, u32[]{:S(2)}, u32[]{:S(2)}) collective-permute-start(bf16[4,1,256]{2,1,0:T(2,128)(2,1)S(1)} %get-tuple-element.18), channel_id=1, source_target_pairs={{0,1},{1,2},{2,3},{4,5},{5,6},{6,7},{8,9},{9,10},{10,11},{12,13},{... | collective-permute-start | bytes 6152 | tf_op jit(solution)/shard_map/ppermute | solution.py:17
  43.0 1.3 fusion.77
  45.6 5.4 %collective-permute-start.4 = (bf16[1,64,256]{2,1,0:T(8,128)(2,1)S(1)}, bf16[1,64,256]{2,1,0:T(8,128)(2,1)S(1)}, u32[]{:S(2)}, u32[]{:S(2)}) collective-permute-start(bf16[1,64,256]{2,1,0:T(8,128)(2,1)S(1)} %get-tuple-element.22), channel_id=1, source_target_pairs={{0,4},{4,8},{8,12},{12,16},{16,20},{20,24},{24,28},{1,5},{5,9},{9,... | collective-permute-start | bytes 98312 | tf_op jit(solution)/shard_map/ppermute | solution.py:17
  53.9 3.5 %collective-permute-start.6 = (bf16[4,1,256]{2,1,0:T(2,128)(2,1)S(1)}, bf16[4,1,256]{2,1,0:T(2,128)(2,1)S(1)}, u32[]{:S(2)}, u32[]{:S(2)}) collective-permute-start(bf16[4,1,256]{2,1,0:T(2,128)(2,1)S(1)} %get-tuple-element.16), channel_id=1, source_target_pairs={{0,1},{1,2},{2,3},{4,5},{5,6},{6,7},{8,9},{9,10},{10,11},{12,13},{... | collective-permute-start | bytes 6152 | tf_op jit(solution)/shard_map/ppermute | solution.py:17
  59.9 5.2 %collective-permute-start.8 = (bf16[1,64,256]{2,1,0:T(8,128)(2,1)S(1)}, bf16[1,64,256]{2,1,0:T(8,128)(2,1)S(1)}, u32[]{:S(2)}, u32[]{:S(2)}) collective-permute-start(bf16[1,64,256]{2,1,0:T(8,128)(2,1)S(1)} %get-tuple-element.20), channel_id=1, source_target_pairs={{0,4},{4,8},{8,12},{12,16},{16,20},{20,24},{24,28},{1,5},{5,9},{9,... | collective-permute-start | bytes 98312 | tf_op jit(solution)/shard_map/ppermute | solution.py:17
  65.3 1.4 collective-permute-done.8
  68.0 4.5 %collective-permute-start.10 = (bf16[4,1,256]{2,1,0:T(2,128)(2,1)S(1)}, bf16[4,1,256]{2,1,0:T(2,128)(2,1)S(1)}, u32[]{:S(2)}, u32[]{:S(2)}) collective-permute-start(bf16[4,1,256]{2,1,0:T(2,128)(2,1)S(1)} %get-tuple-element.14), channel_id=1, source_target_pairs={{0,1},{1,2},{2,3},{4,5},{5,6},{6,7},{8,9},{9,10},{10,11},{12,13},{... | collective-permute-start | bytes 6152 | tf_op jit(solution)/shard_map/ppermute | solution.py:17
  74.3 3.9 %gather_fusion = bf16[1024,256]{1,0:T(8,128)(2,1)S(1)} fusion(bf16[128,256]{1,0:T(8,128)(2,1)S(1)} %bitcast.84, s32[1024]{0:T(1024)S(1)} %broadcast_clamp_fusion.1), kind=kCustom, calls=%fused_computation | custom fusion | bytes 1052672 | tf_op jit(solution)/shard_map/jit(_take)/gather | solution.py:84
  79.2 6.5 %all-to-all-start.1 = ((f32[4,3,256]{2,1,0:T(4,128)}), f32[4,3,256]{2,1,0:T(4,128)S(1)}, u32[]{:S(2)}, u32[]{:S(2)}) async-start(f32[4,3,256]{2,1,0:T(4,128)} %fusion.11), calls=%async_computation.1 | async-start | bytes 32768 | tf_op jit(solution)/shard_map/all_to_all | solution.py:96
  85.7 3.8 %all-to-all-done.1 = f32[4,3,256]{2,1,0:T(4,128)S(1)} async-done(((f32[4,3,256]{2,1,0:T(4,128)}), f32[4,3,256]{2,1,0:T(4,128)S(1)}, u32[]{:S(2)}, u32[]{:S(2)}) %all-to-all-start.1) | async-done | bytes 12320 | tf_op jit(solution)/shard_map/all_to_all | solution.py:96
  89.8 8.2 %scatter_custom_fusion = f32[3,8192]{0,1:T(8,128)} fusion(s32[1024]{0:T(1024)S(1)} %bitcast.95, f32[1024,3]{1,0:T(8,128)S(1)} %copy.23, f32[]{:T(128)} %constant.9.clone.1), kind=kCustom, calls=%fused_computation.3 | custom fusion | flops 3072 | bytes 98308 | tf_op jit(solution)/shard_map/scatter-add | solution.py:100
  98.0 3.5 %copy.24 = f32[3,64,128]{2,1,0:T(8,128)} copy(f32[3,64,128]{0,2,1:T(8,128)} %bitcast.86) | data formatting | bytes 196608 | tf_op jit(solution)/shard_map/reshape | solution.py:102
  101.6 73.6 %all-reduce.4.cloned.1.call-done = f32[3,64,128]{2,1,0:T(8,128)} async-done(((f32[3,64,128]{2,1,0:T(8,128)}), f32[3,64,128]{2,1,0:T(8,128)}) %all-reduce.4.cloned.1.call-update) | async-done | bytes 98320 | tf_op jit(solution)/shard_map/psum | solution.py:101
  176.2 2.6 copy.25
  178.8 103.9 %all_gather.3 = f32[3,32768]{0,1:T(8,128)} all-gather(f32[3,8192]{0,1:T(8,128)} %bitcast.85), channel_id=1, replica_groups=mesh['slab'=8,'patch'=4] {'patch'}, dimensions={1}, use_global_device_ids=true | all-gather | bytes 491520 | tf_op jit(solution)/shard_map/all_gather | solution.py:107
  282.7 8.6 %gather_fusion.1 = f32[1024,3]{1,0:T(8,128)S(1)} fusion(f32[3,32768]{0,1:T(8,128)} %all_gather.3, s32[1024]{0:T(1024)S(1)} %broadcast_clamp_fusion), kind=kCustom, calls=%fused_computation.1 | custom fusion | bytes 28672 | tf_op jit(solution)/shard_map/gather | solution.py:108
  (82 shorter events, 23.0 us)
Async XLA Ops:
  7.2 51.1 %copy-start.6 = (f32[2,64]{1,0:T(2,128)S(1)}, f32[2,64]{1,0:T(2,128)}, u32[]{:S(2)}) copy-start(f32[2,64]{1,0:T(2,128)} %param.15) | copy-start | bytes 1540
  7.2 57.9 %copy-start.1 = (bf16[256,256]{1,0:T(8,128)(2,1)S(1)}, bf16[256,256]{1,0:T(8,128)(2,1)}, u32[]{:S(2)}) copy-start(bf16[256,256]{1,0:T(8,128)(2,1)} %param.16) | copy-start | bytes 393220
  8.3 28.0 %collective-permute-start.1 = (bf16[1,64,256]{2,1,0:T(8,128)(2,1)S(1)}, bf16[1,64,256]{2,1,0:T(8,128)(2,1)S(1)}, u32[]{:S(2)}, u32[]{:S(2)}) collective-permute-start(bf16[1,64,256]{2,1,0:T(8,128)(2,1)S(1)} %get-tuple-element.25), channel_id=1, source_target_pairs={{4,0},{8,4},{12,8},{16,12},{20,16},{24,20},{28,24},{5,1},{9,5},{13... | collective-permute-start | bytes 98312 | tf_op jit(solution)/shard_map/ppermute | solution.py:19
  9.6 26.7 %collective-permute-start = (bf16[1,64,256]{2,1,0:T(8,128)(2,1)S(1)}, bf16[1,64,256]{2,1,0:T(8,128)(2,1)S(1)}, u32[]{:S(2)}, u32[]{:S(2)}) collective-permute-start(bf16[1,64,256]{2,1,0:T(8,128)(2,1)S(1)} %get-tuple-element.24), channel_id=1, source_target_pairs={{0,4},{4,8},{8,12},{12,16},{16,20},{20,24},{24,28},{1,5},{5,9},{9,... | collective-permute-start | bytes 98312 | tf_op jit(solution)/shard_map/ppermute | solution.py:17
  15.1 64.1 %all-to-all-start = ((s32[4,1,256]{2,1,0:T(1,128)}), s32[4,1,256]{2,1,0:T(1,128)S(1)}, u32[]{:S(2)}, u32[]{:S(2)}) async-start(s32[4,1,256]{2,1,0:T(1,128)} %bitcast.90), calls=%async_computation | async-start | bytes 8192 | tf_op jit(solution)/shard_map/all_to_all | solution.py:97
  19.3 10.3 %collective-permute-start.13 = (bf16[3,1,128]{2,1,0:T(2,128)(2,1)S(1)}, bf16[3,1,128]{2,1,0:T(2,128)(2,1)S(1)}, u32[]{:S(2)}, u32[]{:S(2)}) collective-permute-start(bf16[3,1,128]{2,1,0:T(2,128)(2,1)S(1)} %get-tuple-element.29), channel_id=1, source_target_pairs={{1,0},{2,1},{3,2},{5,4},{6,5},{7,6},{9,8},{10,9},{11,10},{13,12},{... | collective-permute-start | bytes 2312 | tf_op jit(solution)/shard_map/ppermute | solution.py:19
  20.6 9.0 %collective-permute-start.12 = (bf16[3,1,128]{2,1,0:T(2,128)(2,1)S(1)}, bf16[3,1,128]{2,1,0:T(2,128)(2,1)S(1)}, u32[]{:S(2)}, u32[]{:S(2)}) collective-permute-start(bf16[3,1,128]{2,1,0:T(2,128)(2,1)S(1)} %get-tuple-element.28), channel_id=1, source_target_pairs={{0,1},{1,2},{2,3},{4,5},{5,6},{6,7},{8,9},{9,10},{10,11},{12,13},{... | collective-permute-start | bytes 2312 | tf_op jit(solution)/shard_map/ppermute | solution.py:17
  30.7 70.8 %collective-permute-start.15 = (bf16[3,1,128]{2,1,0:T(2,128)(2,1)S(1)}, bf16[3,1,128]{2,1,0:T(2,128)(2,1)S(1)}, u32[]{:S(2)}, u32[]{:S(2)}) collective-permute-start(bf16[3,1,128]{2,1,0:T(2,128)(2,1)S(1)} %get-tuple-element.27), channel_id=1, source_target_pairs={{1,0},{2,1},{3,2},{5,4},{6,5},{7,6},{9,8},{10,9},{11,10},{13,12},{... | collective-permute-start | bytes 2312 | tf_op jit(solution)/shard_map/ppermute | solution.py:19
  32.0 69.6 %collective-permute-start.14 = (bf16[3,1,128]{2,1,0:T(2,128)(2,1)S(1)}, bf16[3,1,128]{2,1,0:T(2,128)(2,1)S(1)}, u32[]{:S(2)}, u32[]{:S(2)}) collective-permute-start(bf16[3,1,128]{2,1,0:T(2,128)(2,1)S(1)} %get-tuple-element.26), channel_id=1, source_target_pairs={{0,1},{1,2},{2,3},{4,5},{5,6},{6,7},{8,9},{9,10},{10,11},{12,13},{... | collective-permute-start | bytes 2312 | tf_op jit(solution)/shard_map/ppermute | solution.py:17
  36.3 6.7 %collective-permute-start.3 = (bf16[4,1,256]{2,1,0:T(2,128)(2,1)S(1)}, bf16[4,1,256]{2,1,0:T(2,128)(2,1)S(1)}, u32[]{:S(2)}, u32[]{:S(2)}) collective-permute-start(bf16[4,1,256]{2,1,0:T(2,128)(2,1)S(1)} %get-tuple-element.19), channel_id=1, source_target_pairs={{1,0},{2,1},{3,2},{5,4},{6,5},{7,6},{9,8},{10,9},{11,10},{13,12},{... | collective-permute-start | bytes 6152 | tf_op jit(solution)/shard_map/ppermute | solution.py:19
  37.6 5.4 %collective-permute-start.2 = (bf16[4,1,256]{2,1,0:T(2,128)(2,1)S(1)}, bf16[4,1,256]{2,1,0:T(2,128)(2,1)S(1)}, u32[]{:S(2)}, u32[]{:S(2)}) collective-permute-start(bf16[4,1,256]{2,1,0:T(2,128)(2,1)S(1)} %get-tuple-element.18), channel_id=1, source_target_pairs={{0,1},{1,2},{2,3},{4,5},{5,6},{6,7},{8,9},{9,10},{10,11},{12,13},{... | collective-permute-start | bytes 6152 | tf_op jit(solution)/shard_map/ppermute | solution.py:17
  44.3 7.8 %collective-permute-start.5 = (bf16[1,64,256]{2,1,0:T(8,128)(2,1)S(1)}, bf16[1,64,256]{2,1,0:T(8,128)(2,1)S(1)}, u32[]{:S(2)}, u32[]{:S(2)}) collective-permute-start(bf16[1,64,256]{2,1,0:T(8,128)(2,1)S(1)} %get-tuple-element.23), channel_id=1, source_target_pairs={{4,0},{8,4},{12,8},{16,12},{20,16},{24,20},{28,24},{5,1},{9,5},{13... | collective-permute-start | bytes 98312 | tf_op jit(solution)/shard_map/ppermute | solution.py:19
  45.6 7.0 %collective-permute-start.4 = (bf16[1,64,256]{2,1,0:T(8,128)(2,1)S(1)}, bf16[1,64,256]{2,1,0:T(8,128)(2,1)S(1)}, u32[]{:S(2)}, u32[]{:S(2)}) collective-permute-start(bf16[1,64,256]{2,1,0:T(8,128)(2,1)S(1)} %get-tuple-element.22), channel_id=1, source_target_pairs={{0,4},{4,8},{8,12},{12,16},{16,20},{20,24},{24,28},{1,5},{5,9},{9,... | collective-permute-start | bytes 98312 | tf_op jit(solution)/shard_map/ppermute | solution.py:17
  52.6 5.0 %collective-permute-start.7 = (bf16[4,1,256]{2,1,0:T(2,128)(2,1)S(1)}, bf16[4,1,256]{2,1,0:T(2,128)(2,1)S(1)}, u32[]{:S(2)}, u32[]{:S(2)}) collective-permute-start(bf16[4,1,256]{2,1,0:T(2,128)(2,1)S(1)} %get-tuple-element.17), channel_id=1, source_target_pairs={{1,0},{2,1},{3,2},{5,4},{6,5},{7,6},{9,8},{10,9},{11,10},{13,12},{... | collective-permute-start | bytes 6152 | tf_op jit(solution)/shard_map/ppermute | solution.py:19
  53.9 4.3 %collective-permute-start.6 = (bf16[4,1,256]{2,1,0:T(2,128)(2,1)S(1)}, bf16[4,1,256]{2,1,0:T(2,128)(2,1)S(1)}, u32[]{:S(2)}, u32[]{:S(2)}) collective-permute-start(bf16[4,1,256]{2,1,0:T(2,128)(2,1)S(1)} %get-tuple-element.16), channel_id=1, source_target_pairs={{0,1},{1,2},{2,3},{4,5},{5,6},{6,7},{8,9},{9,10},{10,11},{12,13},{... | collective-permute-start | bytes 6152 | tf_op jit(solution)/shard_map/ppermute | solution.py:17
  58.6 6.7 %collective-permute-start.9 = (bf16[1,64,256]{2,1,0:T(8,128)(2,1)S(1)}, bf16[1,64,256]{2,1,0:T(8,128)(2,1)S(1)}, u32[]{:S(2)}, u32[]{:S(2)}) collective-permute-start(bf16[1,64,256]{2,1,0:T(8,128)(2,1)S(1)} %get-tuple-element.21), channel_id=1, source_target_pairs={{4,0},{8,4},{12,8},{16,12},{20,16},{24,20},{28,24},{5,1},{9,5},{13... | collective-permute-start | bytes 98312 | tf_op jit(solution)/shard_map/ppermute | solution.py:19
  59.9 6.8 %collective-permute-start.8 = (bf16[1,64,256]{2,1,0:T(8,128)(2,1)S(1)}, bf16[1,64,256]{2,1,0:T(8,128)(2,1)S(1)}, u32[]{:S(2)}, u32[]{:S(2)}) collective-permute-start(bf16[1,64,256]{2,1,0:T(8,128)(2,1)S(1)} %get-tuple-element.20), channel_id=1, source_target_pairs={{0,4},{4,8},{8,12},{12,16},{16,20},{20,24},{24,28},{1,5},{5,9},{9,... | collective-permute-start | bytes 98312 | tf_op jit(solution)/shard_map/ppermute | solution.py:17
  66.7 6.0 %collective-permute-start.11 = (bf16[4,1,256]{2,1,0:T(2,128)(2,1)S(1)}, bf16[4,1,256]{2,1,0:T(2,128)(2,1)S(1)}, u32[]{:S(2)}, u32[]{:S(2)}) collective-permute-start(bf16[4,1,256]{2,1,0:T(2,128)(2,1)S(1)} %get-tuple-element.15), channel_id=1, source_target_pairs={{1,0},{2,1},{3,2},{5,4},{6,5},{7,6},{9,8},{10,9},{11,10},{13,12},{... | collective-permute-start | bytes 6152 | tf_op jit(solution)/shard_map/ppermute | solution.py:19
  68.0 5.4 %collective-permute-start.10 = (bf16[4,1,256]{2,1,0:T(2,128)(2,1)S(1)}, bf16[4,1,256]{2,1,0:T(2,128)(2,1)S(1)}, u32[]{:S(2)}, u32[]{:S(2)}) collective-permute-start(bf16[4,1,256]{2,1,0:T(2,128)(2,1)S(1)} %get-tuple-element.14), channel_id=1, source_target_pairs={{0,1},{1,2},{2,3},{4,5},{5,6},{6,7},{8,9},{9,10},{10,11},{12,13},{... | collective-permute-start | bytes 6152 | tf_op jit(solution)/shard_map/ppermute | solution.py:17
  79.2 10.4 %all-to-all-start.1 = ((f32[4,3,256]{2,1,0:T(4,128)}), f32[4,3,256]{2,1,0:T(4,128)S(1)}, u32[]{:S(2)}, u32[]{:S(2)}) async-start(f32[4,3,256]{2,1,0:T(4,128)} %fusion.11), calls=%async_computation.1 | async-start | bytes 32768 | tf_op jit(solution)/shard_map/all_to_all | solution.py:96
  85.7 89.5 %all-reduce.4.cloned.1.call-start = ((), (), s32[]{:S(2)}) async-start(), calls=%async_computation.2 | async-start | bytes 196608 | tf_op jit(solution)/shard_map/psum | solution.py:101
  89.8 85.4 %copy-start.3 = (f32[3,64,128]{2,1,0:T(8,128)S(1)}, f32[3,64,128]{2,1,0:T(8,128)}, u32[]{:S(2)}) copy-start(f32[3,64,128]{2,1,0:T(8,128)} %param.24) | copy-start | bytes 294916
  89.8 85.4 %copy-start.5 = (f32[64,128]{1,0:T(8,128)S(1)}, f32[64,128]{1,0:T(8,128)}, u32[]{:S(2)}) copy-start(f32[64,128]{1,0:T(8,128)} %param.25) | copy-start | bytes 98308
  176.2 106.5 %copy-start.4 = (f32[3,64,128]{2,1,0:T(8,128)}, f32[3,64,128]{2,1,0:T(8,128)S(1)}, u32[]{:S(2)}) copy-start(f32[3,64,128]{2,1,0:T(8,128)S(1)} %fusion.33) | copy-start | bytes 294916
  (5 other events, 208.8 us)
Sparse Core Ops, SparseCore 0:
  101.6 73.4 all-reduce.3
where the time goes:
time: 300 us; the launch traced here: 299 us
  blocking collectives  104 us (35%)
  waiting for transfers between devices  80.6 us (27%)
  starting transfers between devices  55.9 us (19%)
  local copies, waits for them, and re-layouts  20.3 us (7%)
  other arithmetic  16.7 us (6%)
  between operations  14.5 us (5%)
  matrix products  7.25 us (2%)
    all_gather x1, blocking collectives, shards(): whole = lax.all_gather(flat_net, 'patch', axis=1, tiled=True)  104 us
    psum x1, waiting for transfers between devices, shards(): loads = lax.psum(local, 'slab')  73.6 us
    ppermute x8, starting transfers between devices, with_halo(): lax.ppermute(tail, axis, [(i, (i + 1) % count) for i in range(ends)])  35.8 us
    ppermute x8, starting transfers between devices, with_halo(): lax.ppermute(head, axis, [((i + 1) % count, i) for i in range(ends)])  10.3 us
    gather x1, local copies, waits for them, and re-layouts, shards(): picked = whole[:, (owner_ids * cells + points).reshape(-1)]  8.57 us
    scatter-add x1, other arithmetic, shards(): local.at[:, got_points.reshape(-1)]  8.21 us
    all_to_all x1, starting transfers between devices, shards(): lax.all_to_all(pull, 'patch', split_axis=0, concat_axis=0, tiled=True)  6.5 us
  transfers between devices with their start and end apart: 19, of which 6 were waited for; matrix products, arithmetic and copies ran while one was open for 10% of the time, Pallas kernels for 0%

commit v1 on v0

--- a/solution.py
+++ b/solution.py
@@ -98,7 +98,7 @@
     )
     local = jnp.zeros((3, cells), jnp.float32)
     local = local.at[:, got_points.reshape(-1)].add(got_pull.transpose(1, 0, 2).reshape(3, -1))
-    loads = lax.psum(local, "slab")
+    loads = jnp.sum(lax.all_gather(local, "slab"), axis=0)
     loads = loads.reshape(3, net_rows, net_cols)
     bend = laplace_net(displacement)
     stiff_term = stiffness[None] * (laplace_net(bend) + 4.0 * bend)

time: 300 us -> 251 us (0.84)
  waiting for transfers between devices: 80.6 us -> 7.76 us
  blocking collectives: 104 us -> 136 us
  between operations: 14.5 us -> 1.15 us
  local copies, waits for them, and re-layouts: 20.3 us -> 25.2 us
    psum x1 -> x0, waiting for transfers between devices: 73.6 us -> none  [shards(): loads = lax.psum(local, 'slab')]
    all_gather x0 -> x1, blocking collectives: none -> 36.5 us  [shards(): loads = jnp.sum(lax.all_gather(local, 'slab'), axis=0)]
    unnamed x25 -> x27, local copies, waits for them, and re-layouts: 1.45 us -> 6.95 us
    all_gather x1, blocking collectives: 104 us -> 99.3 us  [shards(): whole = lax.all_gather(flat_net, 'patch', axis=1, tiled=True)]
  transfers between devices with their start and end apart: 19 -> 18, of which waited for: 6 -> 6; matrix products, arithmetic and copies ran while one was open for 10% -> 7% of each run, Pallas kernels for 0% -> 0%
where the time goes in v1:
time: 251 us; the launch traced here: 250 us
  blocking collectives  136 us (54%)
  starting transfers between devices  56.3 us (22%)
  local copies, waits for them, and re-layouts  25.2 us (10%)
  other arithmetic  16 us (6%)
  waiting for transfers between devices  7.76 us (3%)
  matrix products  7.25 us (3%)
    all_gather x1, blocking collectives, shards(): whole = lax.all_gather(flat_net, 'patch', axis=1, tiled=True)  99.3 us
    all_gather x1, blocking collectives, shards(): loads = jnp.sum(lax.all_gather(local, 'slab'), axis=0)  36.5 us
    ppermute x8, starting transfers between devices, with_halo(): lax.ppermute(tail, axis, [(i, (i + 1) % count) for i in range(ends)])  36.2 us
    ppermute x8, starting transfers between devices, with_halo(): lax.ppermute(head, axis, [((i + 1) % count, i) for i in range(ends)])  10.3 us
    gather x1, local copies, waits for them, and re-layouts, shards(): picked = whole[:, (owner_ids * cells + points).reshape(-1)]  8.57 us
    scatter-add x1, other arithmetic, shards(): local.at[:, got_points.reshape(-1)]  8.2 us
    unnamed x27, local copies, waits for them, and re-layouts  6.95 us
    all_to_all x1, starting transfers between devices, shards(): lax.all_to_all(pull, 'patch', split_axis=0, concat_axis=0, tiled=True)  6.5 us
  transfers between devices with their start and end apart: 18, of which 6 were waited for; matrix products, arithmetic and copies ran while one was open for 7% of the time, Pallas kernels for 0%

profile of v1, /device:TPU:0, one launch (start us, length us, event | category | flops | bytes accessed | tf_op | source)
XLA Modules:
  0.0 249.5 jit_solution(7094669643221390582)
XLA Ops:
  1.7 1.3 collective-permute-start.1
  3.0 5.5 %collective-permute-start = (bf16[1,64,256]{2,1,0:T(8,128)(2,1)S(1)}, bf16[1,64,256]{2,1,0:T(8,128)(2,1)S(1)}, u32[]{:S(2)}, u32[]{:S(2)}) collective-permute-start(bf16[1,64,256]{2,1,0:T(8,128)(2,1)S(1)} %get-tuple-element.24), channel_id=1, source_target_pairs={{0,4},{4,8},{8,12},{12,16},{16,20},{20,24},{24,28},{1,5},{5,9},{9,... | collective-permute-start | bytes 98312 | tf_op jit(solution)/shard_map/ppermute | solution.py:17
  8.6 3.3 %all-to-all-start = ((s32[4,1,256]{2,1,0:T(1,128)}), s32[4,1,256]{2,1,0:T(1,128)S(1)}, u32[]{:S(2)}, u32[]{:S(2)}) async-start(s32[4,1,256]{2,1,0:T(1,128)} %bitcast.92), calls=%async_computation | async-start | bytes 8192 | tf_op jit(solution)/shard_map/all_to_all | solution.py:97
  14.1 3.0 %collective-permute-start.12 = (bf16[3,1,128]{2,1,0:T(2,128)(2,1)S(1)}, bf16[3,1,128]{2,1,0:T(2,128)(2,1)S(1)}, u32[]{:S(2)}, u32[]{:S(2)}) collective-permute-start(bf16[3,1,128]{2,1,0:T(2,128)(2,1)S(1)} %get-tuple-element.28), channel_id=1, source_target_pairs={{0,1},{1,2},{2,3},{4,5},{5,6},{6,7},{8,9},{9,10},{10,11},{12,13},{... | collective-permute-start | bytes 2312 | tf_op jit(solution)/shard_map/ppermute | solution.py:17
  18.3 1.3 reduce.4
  25.4 4.3 %collective-permute-start.14 = (bf16[3,1,128]{2,1,0:T(2,128)(2,1)S(1)}, bf16[3,1,128]{2,1,0:T(2,128)(2,1)S(1)}, u32[]{:S(2)}, u32[]{:S(2)}) collective-permute-start(bf16[3,1,128]{2,1,0:T(2,128)(2,1)S(1)} %get-tuple-element.26), channel_id=1, source_target_pairs={{0,1},{1,2},{2,3},{4,5},{5,6},{6,7},{8,9},{9,10},{10,11},{12,13},{... | collective-permute-start | bytes 2312 | tf_op jit(solution)/shard_map/ppermute | solution.py:17
  31.9 4.2 %collective-permute-start.2 = (bf16[4,1,256]{2,1,0:T(2,128)(2,1)S(1)}, bf16[4,1,256]{2,1,0:T(2,128)(2,1)S(1)}, u32[]{:S(2)}, u32[]{:S(2)}) collective-permute-start(bf16[4,1,256]{2,1,0:T(2,128)(2,1)S(1)} %get-tuple-element.18), channel_id=1, source_target_pairs={{0,1},{1,2},{2,3},{4,5},{5,6},{6,7},{8,9},{9,10},{10,11},{12,13},{... | collective-permute-start | bytes 6152 | tf_op jit(solution)/shard_map/ppermute | solution.py:17
  37.1 1.3 fusion.77
  39.8 5.4 %collective-permute-start.4 = (bf16[1,64,256]{2,1,0:T(8,128)(2,1)S(1)}, bf16[1,64,256]{2,1,0:T(8,128)(2,1)S(1)}, u32[]{:S(2)}, u32[]{:S(2)}) collective-permute-start(bf16[1,64,256]{2,1,0:T(8,128)(2,1)S(1)} %get-tuple-element.22), channel_id=1, source_target_pairs={{0,4},{4,8},{8,12},{12,16},{16,20},{20,24},{24,28},{1,5},{5,9},{9,... | collective-permute-start | bytes 98312 | tf_op jit(solution)/shard_map/ppermute | solution.py:17
  48.1 4.1 %collective-permute-start.6 = (bf16[4,1,256]{2,1,0:T(2,128)(2,1)S(1)}, bf16[4,1,256]{2,1,0:T(2,128)(2,1)S(1)}, u32[]{:S(2)}, u32[]{:S(2)}) collective-permute-start(bf16[4,1,256]{2,1,0:T(2,128)(2,1)S(1)} %get-tuple-element.16), channel_id=1, source_target_pairs={{0,1},{1,2},{2,3},{4,5},{5,6},{6,7},{8,9},{9,10},{10,11},{12,13},{... | collective-permute-start | bytes 6152 | tf_op jit(solution)/shard_map/ppermute | solution.py:17
  54.6 5.2 %collective-permute-start.8 = (bf16[1,64,256]{2,1,0:T(8,128)(2,1)S(1)}, bf16[1,64,256]{2,1,0:T(8,128)(2,1)S(1)}, u32[]{:S(2)}, u32[]{:S(2)}) collective-permute-start(bf16[1,64,256]{2,1,0:T(8,128)(2,1)S(1)} %get-tuple-element.20), channel_id=1, source_target_pairs={{0,4},{4,8},{8,12},{12,16},{16,20},{20,24},{24,28},{1,5},{5,9},{9,... | collective-permute-start | bytes 98312 | tf_op jit(solution)/shard_map/ppermute | solution.py:17
  60.0 1.4 collective-permute-done.8
  62.7 4.5 %collective-permute-start.10 = (bf16[4,1,256]{2,1,0:T(2,128)(2,1)S(1)}, bf16[4,1,256]{2,1,0:T(2,128)(2,1)S(1)}, u32[]{:S(2)}, u32[]{:S(2)}) collective-permute-start(bf16[4,1,256]{2,1,0:T(2,128)(2,1)S(1)} %get-tuple-element.14), channel_id=1, source_target_pairs={{0,1},{1,2},{2,3},{4,5},{5,6},{6,7},{8,9},{9,10},{10,11},{12,13},{... | collective-permute-start | bytes 6152 | tf_op jit(solution)/shard_map/ppermute | solution.py:17
  69.0 3.9 %gather_fusion = bf16[1024,256]{1,0:T(8,128)(2,1)S(1)} fusion(bf16[128,256]{1,0:T(8,128)(2,1)S(1)} %bitcast.85, s32[1024]{0:T(1024)S(1)} %broadcast_clamp_fusion.1), kind=kCustom, calls=%fused_computation | custom fusion | bytes 1052672 | tf_op jit(solution)/shard_map/jit(_take)/gather | solution.py:84
  73.9 6.5 %all-to-all-start.1 = ((f32[4,3,256]{2,1,0:T(4,128)}), f32[4,3,256]{2,1,0:T(4,128)S(1)}, u32[]{:S(2)}, u32[]{:S(2)}) async-start(f32[4,3,256]{2,1,0:T(4,128)} %fusion.11), calls=%async_computation.1 | async-start | bytes 32768 | tf_op jit(solution)/shard_map/all_to_all | solution.py:96
  80.4 3.8 %all-to-all-done.1 = f32[4,3,256]{2,1,0:T(4,128)S(1)} async-done(((f32[4,3,256]{2,1,0:T(4,128)}), f32[4,3,256]{2,1,0:T(4,128)S(1)}, u32[]{:S(2)}, u32[]{:S(2)}) %all-to-all-start.1) | async-done | bytes 12320 | tf_op jit(solution)/shard_map/all_to_all | solution.py:96
  84.5 8.2 %scatter_custom_fusion = f32[3,8192]{0,1:T(8,128)} fusion(s32[1024]{0:T(1024)S(1)} %bitcast.97, f32[1024,3]{1,0:T(8,128)S(1)} %copy.21, f32[]{:T(128)} %constant.9.clone.1), kind=kCustom, calls=%fused_computation.3 | custom fusion | flops 3072 | bytes 98308 | tf_op jit(solution)/shard_map/scatter-add | solution.py:100
  92.7 2.8 %copy.22 = f32[1,3,8192]{2,1,0:T(4,128)S(1)} copy(f32[1,3,8192]{1,2,0:T(8,128)} %bitcast.87) | data formatting | bytes 196608
  95.5 36.5 %all-gather.1 = f32[8,3,8192]{2,1,0:T(4,128)S(1)} all-gather(f32[1,3,8192]{2,1,0:T(4,128)S(1)} %copy.22), channel_id=2, replica_groups=mesh['slab'=8,'patch'=4] {'slab'}, dimensions={0}, use_global_device_ids=true | all-gather | bytes 884736 | tf_op jit(solution)/shard_map/all_gather | solution.py:101
  132.3 2.7 %copy.27 = f32[3,8192]{0,1:T(8,128)} copy(f32[3,8192]{1,0:T(4,128)S(1)} %reduce_sum.9) | data formatting | bytes 196608
  134.9 2.8 %copy.24 = f32[3,64,128]{2,1,0:T(8,128)S(1)} copy(f32[3,64,128]{0,2,1:T(8,128)} %bitcast.88) | data formatting | bytes 196608 | tf_op jit(solution)/shard_map/reshape | solution.py:102
  137.9 2.6 %copy.25 = f32[3,64,128]{0,2,1:T(8,128)} copy(f32[3,64,128]{2,1,0:T(8,128)S(1)} %fusion.33) | data formatting | bytes 196608 | tf_op jit(solution)/shard_map/add | solution.py:105
  140.6 99.3 %all_gather.11 = f32[3,32768]{0,1:T(8,128)} all-gather(f32[3,8192]{0,1:T(8,128)} %bitcast.86), channel_id=1, replica_groups=mesh['slab'=8,'patch'=4] {'patch'}, dimensions={1}, use_global_device_ids=true | all-gather | bytes 491520 | tf_op jit(solution)/shard_map/all_gather | solution.py:107
  239.9 8.6 %gather_fusion.1 = f32[1024,3]{1,0:T(8,128)S(1)} fusion(f32[3,32768]{0,1:T(8,128)} %all_gather.11, s32[1024]{0:T(1024)S(1)} %broadcast_clamp_fusion), kind=kCustom, calls=%fused_computation.1 | custom fusion | bytes 28672 | tf_op jit(solution)/shard_map/gather | solution.py:108
  (83 shorter events, 25.6 us)
Async XLA Ops:
  0.6 52.3 %copy-start.6 = (f32[2,64]{1,0:T(2,128)S(1)}, f32[2,64]{1,0:T(2,128)}, u32[]{:S(2)}) copy-start(f32[2,64]{1,0:T(2,128)} %param.15) | copy-start | bytes 1540
  0.7 59.1 %copy-start.1 = (bf16[256,256]{1,0:T(8,128)(2,1)S(1)}, bf16[256,256]{1,0:T(8,128)(2,1)}, u32[]{:S(2)}) copy-start(bf16[256,256]{1,0:T(8,128)(2,1)} %param.16) | copy-start | bytes 393220
  0.7 51.5 %copy-start.2 = (bf16[256,256]{1,0:T(8,128)(2,1)S(1)}, bf16[256,256]{1,0:T(8,128)(2,1)}, u32[]{:S(2)}) copy-start(bf16[256,256]{1,0:T(8,128)(2,1)} %param.17) | copy-start | bytes 393220
  0.7 52.3 %copy-start.7 = (f32[2,64,256]{2,1,0:T(8,128)S(1)}, f32[2,64,256]{2,1,0:T(8,128)}, u32[]{:S(2)}) copy-start(f32[2,64,256]{2,1,0:T(8,128)} %param.14) | copy-start | bytes 393220
  0.7 52.3 %copy-start.8 = (bf16[256,256]{1,0:T(8,128)(2,1)S(1)}, bf16[256,256]{1,0:T(8,128)(2,1)}, u32[]{:S(2)}) copy-start(bf16[256,256]{1,0:T(8,128)(2,1)} %param.18) | copy-start | bytes 393220
  1.7 28.8 %collective-permute-start.1 = (bf16[1,64,256]{2,1,0:T(8,128)(2,1)S(1)}, bf16[1,64,256]{2,1,0:T(8,128)(2,1)S(1)}, u32[]{:S(2)}, u32[]{:S(2)}) collective-permute-start(bf16[1,64,256]{2,1,0:T(8,128)(2,1)S(1)} %get-tuple-element.25), channel_id=1, source_target_pairs={{4,0},{8,4},{12,8},{16,12},{20,16},{24,20},{28,24},{5,1},{9,5},{13... | collective-permute-start | bytes 98312 | tf_op jit(solution)/shard_map/ppermute | solution.py:19
  3.0 27.5 %collective-permute-start = (bf16[1,64,256]{2,1,0:T(8,128)(2,1)S(1)}, bf16[1,64,256]{2,1,0:T(8,128)(2,1)S(1)}, u32[]{:S(2)}, u32[]{:S(2)}) collective-permute-start(bf16[1,64,256]{2,1,0:T(8,128)(2,1)S(1)} %get-tuple-element.24), channel_id=1, source_target_pairs={{0,4},{4,8},{8,12},{12,16},{16,20},{20,24},{24,28},{1,5},{5,9},{9,... | collective-permute-start | bytes 98312 | tf_op jit(solution)/shard_map/ppermute | solution.py:17
  8.6 65.3 %all-to-all-start = ((s32[4,1,256]{2,1,0:T(1,128)}), s32[4,1,256]{2,1,0:T(1,128)S(1)}, u32[]{:S(2)}, u32[]{:S(2)}) async-start(s32[4,1,256]{2,1,0:T(1,128)} %bitcast.92), calls=%async_computation | async-start | bytes 8192 | tf_op jit(solution)/shard_map/all_to_all | solution.py:97
  12.8 10.3 %collective-permute-start.13 = (bf16[3,1,128]{2,1,0:T(2,128)(2,1)S(1)}, bf16[3,1,128]{2,1,0:T(2,128)(2,1)S(1)}, u32[]{:S(2)}, u32[]{:S(2)}) collective-permute-start(bf16[3,1,128]{2,1,0:T(2,128)(2,1)S(1)} %get-tuple-element.29), channel_id=1, source_target_pairs={{1,0},{2,1},{3,2},{5,4},{6,5},{7,6},{9,8},{10,9},{11,10},{13,12},{... | collective-permute-start | bytes 2312 | tf_op jit(solution)/shard_map/ppermute | solution.py:19
  14.1 9.0 %collective-permute-start.12 = (bf16[3,1,128]{2,1,0:T(2,128)(2,1)S(1)}, bf16[3,1,128]{2,1,0:T(2,128)(2,1)S(1)}, u32[]{:S(2)}, u32[]{:S(2)}) collective-permute-start(bf16[3,1,128]{2,1,0:T(2,128)(2,1)S(1)} %get-tuple-element.28), channel_id=1, source_target_pairs={{0,1},{1,2},{2,3},{4,5},{5,6},{6,7},{8,9},{9,10},{10,11},{12,13},{... | collective-permute-start | bytes 2312 | tf_op jit(solution)/shard_map/ppermute | solution.py:17
  24.1 5.6 %collective-permute-start.15 = (bf16[3,1,128]{2,1,0:T(2,128)(2,1)S(1)}, bf16[3,1,128]{2,1,0:T(2,128)(2,1)S(1)}, u32[]{:S(2)}, u32[]{:S(2)}) collective-permute-start(bf16[3,1,128]{2,1,0:T(2,128)(2,1)S(1)} %get-tuple-element.27), channel_id=1, source_target_pairs={{1,0},{2,1},{3,2},{5,4},{6,5},{7,6},{9,8},{10,9},{11,10},{13,12},{... | collective-permute-start | bytes 2312 | tf_op jit(solution)/shard_map/ppermute | solution.py:19
  25.4 5.1 %collective-permute-start.14 = (bf16[3,1,128]{2,1,0:T(2,128)(2,1)S(1)}, bf16[3,1,128]{2,1,0:T(2,128)(2,1)S(1)}, u32[]{:S(2)}, u32[]{:S(2)}) collective-permute-start(bf16[3,1,128]{2,1,0:T(2,128)(2,1)S(1)} %get-tuple-element.26), channel_id=1, source_target_pairs={{0,1},{1,2},{2,3},{4,5},{5,6},{6,7},{8,9},{9,10},{10,11},{12,13},{... | collective-permute-start | bytes 2312 | tf_op jit(solution)/shard_map/ppermute | solution.py:17
  30.6 6.6 %collective-permute-start.3 = (bf16[4,1,256]{2,1,0:T(2,128)(2,1)S(1)}, bf16[4,1,256]{2,1,0:T(2,128)(2,1)S(1)}, u32[]{:S(2)}, u32[]{:S(2)}) collective-permute-start(bf16[4,1,256]{2,1,0:T(2,128)(2,1)S(1)} %get-tuple-element.19), channel_id=1, source_target_pairs={{1,0},{2,1},{3,2},{5,4},{6,5},{7,6},{9,8},{10,9},{11,10},{13,12},{... | collective-permute-start | bytes 6152 | tf_op jit(solution)/shard_map/ppermute | solution.py:19
  31.9 5.3 %collective-permute-start.2 = (bf16[4,1,256]{2,1,0:T(2,128)(2,1)S(1)}, bf16[4,1,256]{2,1,0:T(2,128)(2,1)S(1)}, u32[]{:S(2)}, u32[]{:S(2)}) collective-permute-start(bf16[4,1,256]{2,1,0:T(2,128)(2,1)S(1)} %get-tuple-element.18), channel_id=1, source_target_pairs={{0,1},{1,2},{2,3},{4,5},{5,6},{6,7},{8,9},{9,10},{10,11},{12,13},{... | collective-permute-start | bytes 6152 | tf_op jit(solution)/shard_map/ppermute | solution.py:17
  38.5 7.8 %collective-permute-start.5 = (bf16[1,64,256]{2,1,0:T(8,128)(2,1)S(1)}, bf16[1,64,256]{2,1,0:T(8,128)(2,1)S(1)}, u32[]{:S(2)}, u32[]{:S(2)}) collective-permute-start(bf16[1,64,256]{2,1,0:T(8,128)(2,1)S(1)} %get-tuple-element.23), channel_id=1, source_target_pairs={{4,0},{8,4},{12,8},{16,12},{20,16},{24,20},{28,24},{5,1},{9,5},{13... | collective-permute-start | bytes 98312 | tf_op jit(solution)/shard_map/ppermute | solution.py:19
  39.8 7.0 %collective-permute-start.4 = (bf16[1,64,256]{2,1,0:T(8,128)(2,1)S(1)}, bf16[1,64,256]{2,1,0:T(8,128)(2,1)S(1)}, u32[]{:S(2)}, u32[]{:S(2)}) collective-permute-start(bf16[1,64,256]{2,1,0:T(8,128)(2,1)S(1)} %get-tuple-element.22), channel_id=1, source_target_pairs={{0,4},{4,8},{8,12},{12,16},{16,20},{20,24},{24,28},{1,5},{5,9},{9,... | collective-permute-start | bytes 98312 | tf_op jit(solution)/shard_map/ppermute | solution.py:17
  46.8 5.6 %collective-permute-start.7 = (bf16[4,1,256]{2,1,0:T(2,128)(2,1)S(1)}, bf16[4,1,256]{2,1,0:T(2,128)(2,1)S(1)}, u32[]{:S(2)}, u32[]{:S(2)}) collective-permute-start(bf16[4,1,256]{2,1,0:T(2,128)(2,1)S(1)} %get-tuple-element.17), channel_id=1, source_target_pairs={{1,0},{2,1},{3,2},{5,4},{6,5},{7,6},{9,8},{10,9},{11,10},{13,12},{... | collective-permute-start | bytes 6152 | tf_op jit(solution)/shard_map/ppermute | solution.py:19
  48.1 4.9 %collective-permute-start.6 = (bf16[4,1,256]{2,1,0:T(2,128)(2,1)S(1)}, bf16[4,1,256]{2,1,0:T(2,128)(2,1)S(1)}, u32[]{:S(2)}, u32[]{:S(2)}) collective-permute-start(bf16[4,1,256]{2,1,0:T(2,128)(2,1)S(1)} %get-tuple-element.16), channel_id=1, source_target_pairs={{0,1},{1,2},{2,3},{4,5},{5,6},{6,7},{8,9},{9,10},{10,11},{12,13},{... | collective-permute-start | bytes 6152 | tf_op jit(solution)/shard_map/ppermute | solution.py:17
  53.3 6.7 %collective-permute-start.9 = (bf16[1,64,256]{2,1,0:T(8,128)(2,1)S(1)}, bf16[1,64,256]{2,1,0:T(8,128)(2,1)S(1)}, u32[]{:S(2)}, u32[]{:S(2)}) collective-permute-start(bf16[1,64,256]{2,1,0:T(8,128)(2,1)S(1)} %get-tuple-element.21), channel_id=1, source_target_pairs={{4,0},{8,4},{12,8},{16,12},{20,16},{24,20},{28,24},{5,1},{9,5},{13... | collective-permute-start | bytes 98312 | tf_op jit(solution)/shard_map/ppermute | solution.py:19
  54.6 6.8 %collective-permute-start.8 = (bf16[1,64,256]{2,1,0:T(8,128)(2,1)S(1)}, bf16[1,64,256]{2,1,0:T(8,128)(2,1)S(1)}, u32[]{:S(2)}, u32[]{:S(2)}) collective-permute-start(bf16[1,64,256]{2,1,0:T(8,128)(2,1)S(1)} %get-tuple-element.20), channel_id=1, source_target_pairs={{0,4},{4,8},{8,12},{12,16},{16,20},{20,24},{24,28},{1,5},{5,9},{9,... | collective-permute-start | bytes 98312 | tf_op jit(solution)/shard_map/ppermute | solution.py:17
  61.4 6.0 %collective-permute-start.11 = (bf16[4,1,256]{2,1,0:T(2,128)(2,1)S(1)}, bf16[4,1,256]{2,1,0:T(2,128)(2,1)S(1)}, u32[]{:S(2)}, u32[]{:S(2)}) collective-permute-start(bf16[4,1,256]{2,1,0:T(2,128)(2,1)S(1)} %get-tuple-element.15), channel_id=1, source_target_pairs={{1,0},{2,1},{3,2},{5,4},{6,5},{7,6},{9,8},{10,9},{11,10},{13,12},{... | collective-permute-start | bytes 6152 | tf_op jit(solution)/shard_map/ppermute | solution.py:19
  62.7 5.4 %collective-permute-start.10 = (bf16[4,1,256]{2,1,0:T(2,128)(2,1)S(1)}, bf16[4,1,256]{2,1,0:T(2,128)(2,1)S(1)}, u32[]{:S(2)}, u32[]{:S(2)}) collective-permute-start(bf16[4,1,256]{2,1,0:T(2,128)(2,1)S(1)} %get-tuple-element.14), channel_id=1, source_target_pairs={{0,1},{1,2},{2,3},{4,5},{5,6},{6,7},{8,9},{9,10},{10,11},{12,13},{... | collective-permute-start | bytes 6152 | tf_op jit(solution)/shard_map/ppermute | solution.py:17
  73.9 10.4 %all-to-all-start.1 = ((f32[4,3,256]{2,1,0:T(4,128)}), f32[4,3,256]{2,1,0:T(4,128)S(1)}, u32[]{:S(2)}, u32[]{:S(2)}) async-start(f32[4,3,256]{2,1,0:T(4,128)} %fusion.11), calls=%async_computation.1 | async-start | bytes 32768 | tf_op jit(solution)/shard_map/all_to_all | solution.py:96
  137.9 102.0 %copy-start.4 = (f32[3,64,128]{2,1,0:T(8,128)}, f32[3,64,128]{2,1,0:T(8,128)S(1)}, u32[]{:S(2)}) copy-start(f32[3,64,128]{2,1,0:T(8,128)S(1)} %fusion.33) | copy-start | bytes 294916
  (4 other events, 68.2 us)
